TPU v7x, 128 devices: a whole 4x4x4 slice. The times are simulated.
128 devices in a mesh: rows: 32 (over y, x, core), cols: 4 (over z).
Axes of the slice: x: 4, y: 4, z: 4, core: 2. Of those that a mesh axis runs over, the one named last changes fastest.
Arguments:
- feats: bfloat16 [131072, 512], P('rows', 'cols'), may hold values from -6 to 6
- adj_vals: bfloat16 [1024, 16, 128, 128], P('rows'), may hold values from -0.125 to 0.125
- colref: int32 [1024, 16], P('rows'), may hold values from 0 to 95, as said below
- fetch_ids: int32 [32, 32, 2], P('rows'), may hold values from -1 to 31, as said below
- w_self: bfloat16 [512, 512], replicated, may hold values from -0.25 to 0.25
- w_neigh: bfloat16 [512, 512], replicated, may hold values from -0.25 to 0.25
- grad_out: bfloat16 [131072, 512], P(('rows', 'cols')), may hold values from -6 to 6
Outputs:
- act_out: bfloat16 [131072, 512], P(('rows', 'cols'))
- grad_self_w: float32 [512, 512], replicated
- grad_neigh_w: float32 [512, 512], replicated
- grad_feats: float32 [131072, 512], P('rows', 'cols')
Inputs may be any that keep to these rules, and one draw needn't show every extreme that they name: `fetch_ids`: entry [r, o, s] is a row tile index within partition o (0 to 31) that partition r reads, or -1 for an empty slot. The entries of one r and o are distinct, all slots with o = r are empty, and every r fills all 2 slots of at least one o. `colref`: entry [b, k], with r = b // 32, is below 32 for partition r's own row tile of that index, or 32 + o * 2 + s for the slot s of fetch_ids[r, o], never an empty slot; so it lies in 0 to 32 + 32 * 2 - 1. The 16 entries of a row tile are distinct and the first is b - r * 32, the row tile itself.
All inputs are finite; a program needn't handle non-finite values.
Results may differ from a plain program's by a relative error of at most 0.0057.
Values may be sent and summed in bfloat16 or wider, within the bound.
A program may use at most 192 MiB of HBM per device.

v0:
```python
import math
import jax
import jax.numpy as jnp
from jax import lax
from jax.sharding import PartitionSpec as P


def body(feats, adj_vals, colref, fetch_ids, w_self, w_neigh, grad_out):
    node_rows, feat_cols = feats.shape
    blocks = adj_vals.shape[0]
    per_block = adj_vals.shape[1]
    tile_rows = adj_vals.shape[2]
    partitions = lax.axis_size("rows")
    capacity = fetch_ids.shape[2]
    total_nodes = node_rows * partitions
    own_tiles = feats.reshape(blocks, tile_rows * feat_cols)
    wanted = lax.all_to_all(fetch_ids, "rows", split_axis=1, concat_axis=0, tiled=True).reshape(
        partitions * capacity
    )
    choose = (wanted[:, None] == jnp.arange(blocks, dtype=jnp.int32)[None, :]).astype(jnp.bfloat16)
    outgoing = jnp.dot(choose, own_tiles, preferred_element_type=jnp.float32).astype(jnp.bfloat16)
    outgoing = outgoing.reshape(partitions, capacity, tile_rows, feat_cols)
    arrived = lax.all_to_all(outgoing, "rows", split_axis=0, concat_axis=0, tiled=True)
    tile_pool = jnp.concatenate(
        [
            feats.reshape(blocks, tile_rows, feat_cols),
            arrived.reshape(partitions * capacity, tile_rows, feat_cols),
        ],
        axis=0,
    )
    picked = jnp.take(tile_pool, colref, axis=0)
    aggregated = jnp.einsum("bkij,bkjf->bif", adj_vals, picked, preferred_element_type=jnp.float32)
    aggregated = aggregated.astype(jnp.bfloat16).reshape(node_rows, feat_cols)
    feat_rows, agg_rows = (
        lax.all_to_all(feats, "cols", split_axis=0, concat_axis=1, tiled=True),
        lax.all_to_all(aggregated, "cols", split_axis=0, concat_axis=1, tiled=True),
    )
    preact = jnp.dot(feat_rows, w_self, preferred_element_type=jnp.float32) + jnp.dot(
        agg_rows, w_neigh, preferred_element_type=jnp.float32
    )
    activation, pull_back = jax.vjp(jax.nn.gelu, preact)
    grad_pre = pull_back(grad_out.astype(jnp.float32))[0].astype(jnp.bfloat16)
    contract = (((0,), (0,)), ((), ()))
    weight_terms = (
        lax.dot_general(feat_rows, grad_pre, contract, preferred_element_type=jnp.float32),
        lax.dot_general(agg_rows, grad_pre, contract, preferred_element_type=jnp.float32),
    )
    self_sum, neigh_sum = lax.psum((weight_terms[0], weight_terms[1]), ("rows", "cols"))
    grad_scale = 1.0 / math.sqrt(total_nodes)
    grad_self_w = self_sum * grad_scale
    grad_neigh_w = neigh_sum * grad_scale
    dims_back = (((1,), (1,)), ((), ()))
    column = lax.axis_index("cols") * feat_cols
    self_slice = lax.dynamic_slice_in_dim(w_self, column, feat_cols, 0)
    neigh_slice = lax.dynamic_slice_in_dim(w_neigh, column, feat_cols, 0)
    rows_in = lax.all_gather(grad_pre, "cols", axis=0, tiled=True)
    self_cols = lax.dot_general(rows_in, self_slice, dims_back, preferred_element_type=jnp.float32)
    neigh_cols = lax.dot_general(
        rows_in, neigh_slice, dims_back, preferred_element_type=jnp.float32
    )
    stacked = jnp.concatenate([self_cols, neigh_cols], axis=1).astype(jnp.bfloat16)
    self_part = stacked[:, :feat_cols]
    grad_agg = stacked[:, feat_cols:]
    grad_blocks = grad_agg.reshape(blocks, tile_rows, feat_cols)
    per_ref = jnp.einsum(
        "bkij,bif->bkjf", adj_vals, grad_blocks, preferred_element_type=jnp.float32
    )
    pool_slots = blocks + partitions * capacity
    pick_table = (
        jnp.arange(pool_slots, dtype=jnp.int32)[:, None] == colref.reshape(1, blocks * per_block)
    ).astype(jnp.float32)
    pooled = jnp.dot(
        pick_table,
        per_ref.reshape(blocks * per_block, tile_rows * feat_cols),
        precision=lax.Precision.HIGHEST,
        preferred_element_type=jnp.float32,
    )
    shares = pooled.astype(jnp.bfloat16).reshape(pool_slots, tile_rows, feat_cols)
    remote_shares = shares[blocks:].reshape(partitions, capacity, tile_rows, feat_cols)
    returned = lax.all_to_all(remote_shares, "rows", split_axis=0, concat_axis=0, tiled=True)
    gathered_back = jnp.dot(
        choose.T,
        returned.reshape(partitions * capacity, tile_rows * feat_cols),
        preferred_element_type=jnp.float32,
    )
    grad_feats = self_part.astype(jnp.float32) + shares[:blocks].astype(jnp.float32).reshape(
        node_rows, feat_cols
    )
    grad_feats = grad_feats + gathered_back.reshape(node_rows, feat_cols)
    return (activation.astype(jnp.bfloat16), grad_self_w, grad_neigh_w, grad_feats)


def solution(mesh):
    in_specs = (
        P("rows", "cols"),
        P("rows", None, None, None),
        P("rows", None),
        P("rows", None, None),
        P(),
        P(),
        P(("rows", "cols"), None),
    )
    out_specs = (P(("rows", "cols"), None), P(), P(), P("rows", "cols"))
    return jax.shard_map(body, mesh=mesh, in_specs=in_specs, out_specs=out_specs, check_vma=False)
```

profile of v0, /device:TPU:0, one launch (start us, length us, event | category | flops | bytes accessed | tf_op | source)
XLA Modules:
  0.0 468.5 jit_solution(2527435484349896378)
XLA Ops:
  9.4 7.4 %all-to-all-start.1 = ((s32[1,32,2]{2,0,1:T(1,128)}), s32[1,32,2]{2,0,1:T(1,128)S(1)}, u32[]{:S(2)}, u32[]{:S(2)}) async-start(s32[1,32,2]{2,0,1:T(1,128)} %copy.40), calls=%async_computation.1 | async-start | bytes 32768 | tf_op jit(solution)/shard_map/all_to_all | solution.py:17
  16.8 1.5 reshape.64
  18.4 5.7 %all-to-all-done.1 = s32[1,32,2]{2,0,1:T(1,128)S(1)} async-done(((s32[1,32,2]{2,0,1:T(1,128)}), s32[1,32,2]{2,0,1:T(1,128)S(1)}, u32[]{:S(2)}, u32[]{:S(2)}) %all-to-all-start.1) | async-done | bytes 288 | tf_op jit(solution)/shard_map/all_to_all | solution.py:17
  26.2 1.9 copy.54
  28.1 4.1 all-to-all-start.2
  32.5 29.7 %all-to-all-done.2 = bf16[32,2,128,128]{3,2,1,0:T(8,128)(2,1)S(1)} async-done(((bf16[32,2,128,128]{3,2,1,0:T(8,128)(2,1)}), bf16[32,2,128,128]{3,2,1,0:T(8,128)(2,1)S(1)}, u32[]{:S(2)}, u32[]{:S(2)}) %all-to-all-start.2) | async-done | bytes 2097184 | tf_op jit(solution)/shard_map/all_to_all | solution.py:23
  62.2 5.3 %all-to-all-start = ((bf16[4,1024,128]{2,1,0:T(8,128)(2,1)}), bf16[4,1024,128]{2,1,0:T(8,128)(2,1)}, u32[]{:S(2)}, u32[]{:S(2)}) async-start(bf16[4,1024,128]{2,1,0:T(8,128)(2,1)} %bitcast), calls=%async_computation | async-start | bytes 2097152 | tf_op jit(solution)/shard_map/all_to_all | solution.py:35
  67.5 3.2 pad_maximum_fusion
  70.7 15.8 %gather_fusion = bf16[512,128,128]{2,1,0:T(8,128)(2,1)} fusion(bf16[96,128,128]{2,1,0:T(8,128)(2,1)} %pad_maximum_fusion, s32[1024]{0:T(1024)S(1)} %pad_clamp_fusion), kind=kCustom, calls=%fused_computation | custom fusion | bytes 33556480 | tf_op jit(solution)/shard_map/jit(_take)/gather | solution.py:31
  86.5 13.0 %bitcast_convert_fusion = bf16[32,128,128]{1,2,0:T(8,128)(2,1)S(1)} fusion(bf16[32,16,128,128]{3,2,1,0:T(8,128)(2,1)} %param.8, bf16[32,16,128,128]{3,2,1,0:T(8,128)(2,1)} %bitcast.60, pred[32,16]{1,0:T(8,128)(4,1)S(1)} %copy.39), kind=kOutput, calls=%fused_computation.35 | convolution fusion | flops 2156396544 | bytes 34603520 | tf_op jit(solution)/shard_map/bkij,bkjf->bif/dot_general | solution.py:32
  100.8 4.9 %all-to-all-start.3 = ((bf16[4,1024,128]{1,2,0:T(8,128)(2,1)}), bf16[4,1024,128]{1,2,0:T(8,128)(2,1)S(1)}, u32[]{:S(2)}, u32[]{:S(2)}) async-start(bf16[4,1024,128]{1,2,0:T(8,128)(2,1)} %copy.42), calls=%async_computation.3 | async-start | bytes 2097152 | tf_op jit(solution)/shard_map/all_to_all | solution.py:36
  105.8 1.5 copy.38
  107.3 2.1 fusion.37
  109.3 9.3 %all-to-all-done.3 = bf16[4,1024,128]{1,2,0:T(8,128)(2,1)S(1)} async-done(((bf16[4,1024,128]{1,2,0:T(8,128)(2,1)}), bf16[4,1024,128]{1,2,0:T(8,128)(2,1)S(1)}, u32[]{:S(2)}, u32[]{:S(2)}) %all-to-all-start.3) | async-done | bytes 1048608 | tf_op jit(solution)/shard_map/all_to_all | solution.py:36
  119.6 5.4 %fusion.15 = (bf16[1024,512]{1,0:T(8,128)(2,1)S(1)}, bf16[1024,512]{1,0:T(8,128)(2,1)}) fusion(bf16[1024,512]{1,0:T(8,128)(2,1)} %param.13, f32[1024,512]{1,0:T(8,128)} %fusion.37, bf16[1024,512]{0,1:T(8,128)(2,1)} %bitcast.66, bf16[512,512]{1,0:T(8,128)(2,1)S(1)} %copy-done), kind=kOutput, calls=%fused_computation.23 | convolution fusion | flops 549453824 | bytes 6815744 | tf_op jit(solution)/shard_map/dot_general | solution.py:38
  125.0 1.7 convolution_bitcast_fusion.1
  126.7 1.7 fusion.38
  129.2 174.5 %all-reduce.3.cloned.1.call-done = (f32[512,512]{0,1:T(8,128)}, f32[512,512]{0,1:T(8,128)}) async-done(((f32[512,512]{0,1:T(8,128)}, f32[512,512]{0,1:T(8,128)}), (f32[512,512]{0,1:T(8,128)}, f32[512,512]{0,1:T(8,128)})) %all-reduce.3.cloned.1.call-update) | async-done | bytes 2097168 | tf_op jit(solution)/shard_map/psum | solution.py:48
  303.7 1.8 broadcast_multiply_fusion
  308.1 3.4 convolution_convert_fusion.1
  311.6 21.4 %convolution_bitcast_fusion = f32[32,16,128,128]{2,3,1,0:T(8,128)} fusion(bf16[32,128,128,1]{2,1,3,0:T(8,128)(2,1)S(1)} %bitcast.63, bf16[32,16,128,128]{3,2,1,0:T(8,128)(2,1)} %param.8), kind=kOutput, calls=%fused_computation.9 | convolution fusion | flops 2147483648 | bytes 51380224 | tf_op jit(solution)/shard_map/bkij,bif->bkjf/dot_general | solution.py:65
  333.0 33.4 %copy.46 = f32[32,16,128,128]{3,2,1,0:T(8,128)} copy(f32[32,16,128,128]{2,3,1,0:T(8,128)} %convolution_bitcast_fusion) | data formatting | bytes 67108864 | tf_op jit(solution)/shard_map/bkij,bif->bkjf/dot_general | solution.py:65
  366.4 42.4 %fusion.3 = bf16[96,16384]{1,0:T(8,128)(2,1)} fusion(f32[64,8,128,128]{3,2,1,0:T(8,128)} %bitcast.59, s32[512]{0:T(512)S(1)} %eq.35), kind=kOutput, calls=%fused_computation.4 | convolution fusion | flops 9665298432 | bytes 36702208 | tf_op jit(solution)/shard_map/dot_general | solution.py:72
  408.8 1.7 slice_bitcast_fusion
  410.5 1.9 copy.56
  412.4 6.0 %all-to-all-start.4 = ((bf16[32,2,128,128]{3,2,1,0:T(8,128)(2,1)}), bf16[32,2,128,128]{3,2,1,0:T(8,128)(2,1)}, u32[]{:S(2)}, u32[]{:S(2)}) async-start(bf16[32,2,128,128]{3,2,1,0:T(8,128)(2,1)} %bitcast.29), calls=%async_computation.4 | async-start | bytes 4194304 | tf_op jit(solution)/shard_map/all_to_all | solution.py:80
  418.4 2.7 slice_convert_fusion
  421.1 1.7 reshape.72
  422.8 25.6 %all-to-all-done.4 = bf16[32,2,128,128]{3,2,1,0:T(8,128)(2,1)} async-done(((bf16[32,2,128,128]{3,2,1,0:T(8,128)(2,1)}), bf16[32,2,128,128]{3,2,1,0:T(8,128)(2,1)}, u32[]{:S(2)}, u32[]{:S(2)}) %all-to-all-start.4) | async-done | bytes 2097184 | tf_op jit(solution)/shard_map/all_to_all | solution.py:80
  448.4 4.4 fusion.23
  452.8 2.7 reshape.71
  455.5 5.5 %fusion.12 = f32[4096,128]{1,0:T(8,128)} fusion(f32[4096,128]{1,0:T(8,128)} %reshape.71, f32[4096,128]{1,0:T(8,128)S(1)} %reshape.72, bf16[4096,512]{1,0:T(8,128)(2,1)} %all-gather.2.cloned.1.call-done, bf16[512,512]{1,0:T(8,128)(2,1)S(1)} %copy-done.5, s32[]{:T(128)S(6)} %select_n.15), kind=kOutput, calls=%fused_computation.15 | convolution fusion | flops 538968064 | bytes 10616836 | tf_op jit(solution)/shard_map/dot_general | solution.py:57
  (36 shorter events, 9.4 us)
Async XLA Ops:
  8.0 111.6 %copy-start = (bf16[512,512]{1,0:T(8,128)(2,1)S(1)}, bf16[512,512]{1,0:T(8,128)(2,1)}, u32[]{:S(2)}) copy-start(bf16[512,512]{1,0:T(8,128)(2,1)} %param.12) | copy-start | bytes 1572868
  9.4 14.7 %all-to-all-start.1 = ((s32[1,32,2]{2,0,1:T(1,128)}), s32[1,32,2]{2,0,1:T(1,128)S(1)}, u32[]{:S(2)}, u32[]{:S(2)}) async-start(s32[1,32,2]{2,0,1:T(1,128)} %copy.40), calls=%async_computation.1 | async-start | bytes 32768 | tf_op jit(solution)/shard_map/all_to_all | solution.py:17
  28.1 4.2 copy-start.6
  28.1 34.1 %all-to-all-start.2 = ((bf16[32,2,128,128]{3,2,1,0:T(8,128)(2,1)}), bf16[32,2,128,128]{3,2,1,0:T(8,128)(2,1)S(1)}, u32[]{:S(2)}, u32[]{:S(2)}) async-start(bf16[32,2,128,128]{3,2,1,0:T(8,128)(2,1)} %bitcast.62), calls=%async_computation.2 | async-start | bytes 4194304 | tf_op jit(solution)/shard_map/all_to_all | solution.py:23
  62.2 38.6 %all-to-all-start = ((bf16[4,1024,128]{2,1,0:T(8,128)(2,1)}), bf16[4,1024,128]{2,1,0:T(8,128)(2,1)}, u32[]{:S(2)}, u32[]{:S(2)}) async-start(bf16[4,1024,128]{2,1,0:T(8,128)(2,1)} %bitcast), calls=%async_computation | async-start | bytes 2097152 | tf_op jit(solution)/shard_map/all_to_all | solution.py:35
  100.8 6.4 %copy-start.5 = (bf16[512,512]{1,0:T(8,128)(2,1)S(1)}, bf16[512,512]{1,0:T(8,128)(2,1)}, u32[]{:S(2)}) copy-start(bf16[512,512]{1,0:T(8,128)(2,1)} %param.11) | copy-start | bytes 1572868
  100.8 17.8 %all-to-all-start.3 = ((bf16[4,1024,128]{1,2,0:T(8,128)(2,1)}), bf16[4,1024,128]{1,2,0:T(8,128)(2,1)S(1)}, u32[]{:S(2)}, u32[]{:S(2)}) async-start(bf16[4,1024,128]{1,2,0:T(8,128)(2,1)} %copy.42), calls=%async_computation.3 | async-start | bytes 2097152 | tf_op jit(solution)/shard_map/all_to_all | solution.py:36
  105.8 198.0 %all-reduce.3.cloned.1.call-start = ((), (), s32[]{:S(2)}) async-start(), calls=%async_computation.6 | async-start | bytes 4194304 | tf_op jit(solution)/shard_map/psum | solution.py:48
  118.6 1.0 copy-start.3
  125.0 3.5 copy-start.2
  125.0 1.7 copy-start.4
  128.5 179.7 %all-gather.2.cloned.1.call-start = ((), (), s32[]{:S(2)}) async-start(), calls=%async_computation.5 | async-start | bytes 5242880 | tf_op jit(solution)/shard_map/all_gather | solution.py:56
  412.4 35.9 %all-to-all-start.4 = ((bf16[32,2,128,128]{3,2,1,0:T(8,128)(2,1)}), bf16[32,2,128,128]{3,2,1,0:T(8,128)(2,1)}, u32[]{:S(2)}, u32[]{:S(2)}) async-start(bf16[32,2,128,128]{3,2,1,0:T(8,128)(2,1)} %bitcast.29), calls=%async_computation.4 | async-start | bytes 4194304 | tf_op jit(solution)/shard_map/all_to_all | solution.py:80
  455.5 5.5 %copy-start.1 = (bf16[512,512]{1,0:T(8,128)(2,1)S(1)}, bf16[512,512]{1,0:T(8,128)(2,1)}, u32[]{:S(2)}) copy-start(bf16[512,512]{1,0:T(8,128)(2,1)} %param.12) | copy-start | bytes 1572868
Sparse Core Ops, SparseCore 0:
  128.6 175.0 all-reduce.2
Sparse Core Ops, SparseCore 1:
  131.2 46.4 all-gather.1
where the time goes:
time: 470 us; the launch traced here: 468 us
  waiting for transfers between devices  245 us (52%)
  matrix products  102 us (22%)
  local copies, waits for them, and re-layouts  69.5 us (15%)
  starting transfers between devices  27.8 us (6%)
  between operations  15.6 us (3%)
  other arithmetic  8.32 us (2%)
    psum x1, waiting for transfers between devices, body(): lax.psum((weight_terms[0], weight_terms[1]), ('rows', 'cols'))  175 us
    dot_general x1, matrix products, body(): jnp.dot(pick_table, per_ref.reshape(blocks * per_block, tile_rows * feat_...  42.4 us
    dot_general x1, local copies, waits for them, and re-layouts, body(): jnp.einsum('bkij,bif->bkjf', adj_vals, grad_blocks, preferred_element_typ...  33.4 us
    all_to_all x1, waiting for transfers between devices, body(): lax.all_to_all(outgoing, 'rows', split_axis=0, concat_axis=0, tiled=True)  29.7 us
    all_to_all x1, waiting for transfers between devices, body(): lax.all_to_all(remote_shares, 'rows', split_axis=0, concat_axis=0, tiled=...  25.6 us
    dot_general x1, matrix products, body(): jnp.einsum('bkij,bif->bkjf', adj_vals, grad_blocks, preferred_element_typ...  21.4 us
    gather x1, local copies, waits for them, and re-layouts, body(): picked = jnp.take(tile_pool, colref, axis=0)  15.8 us
    dot_general x1, matrix products, body(): jnp.einsum('bkij,bkjf->bif', adj_vals, picked, preferred_element_type=jnp...  13 us
  transfers between devices with their start and end apart: 7, of which 5 were waited for; matrix products, arithmetic and copies ran while one was open for 10% of the time, Pallas kernels for 0%

commit v1 on v0

--- a/solution.py
+++ b/solution.py
@@ -45,7 +45,7 @@
         lax.dot_general(feat_rows, grad_pre, contract, preferred_element_type=jnp.float32),
         lax.dot_general(agg_rows, grad_pre, contract, preferred_element_type=jnp.float32),
     )
-    self_sum, neigh_sum = lax.psum((weight_terms[0], weight_terms[1]), ("rows", "cols"))
+    self_sum, neigh_sum = lax.psum(lax.psum((weight_terms[0], weight_terms[1]), "rows"), "cols")
     grad_scale = 1.0 / math.sqrt(total_nodes)
     grad_self_w = self_sum * grad_scale
     grad_neigh_w = neigh_sum * grad_scale

time: 470 us -> 506 us (1.077)
  waiting for transfers between devices: 245 us -> 282 us
    all_gather x1, waiting for transfers between devices: 0.01 us -> 46.1 us  [body(): rows_in = lax.all_gather(grad_pre, 'cols', axis=0, tiled=True)]
    psum x1 -> x2, waiting for transfers between devices: 175 us -> 165 us  [the longest x1 105 us: body(): lax.psum((weight_terms[0], weight_terms[1]), 'rows')]
  transfers between devices with their start and end apart: 7 -> 8, of which waited for: 5 -> 7; matrix products, arithmetic and copies ran while one was open for 10% -> 9% of each run, Pallas kernels for 0% -> 0%
where the time goes in v1:
time: 506 us; the launch traced here: 505 us
  waiting for transfers between devices  282 us (56%)
  matrix products  102 us (20%)
  local copies, waits for them, and re-layouts  69.5 us (14%)
  starting transfers between devices  29.1 us (6%)
  between operations  13.9 us (3%)
  other arithmetic  8.32 us (2%)
    psum x1, waiting for transfers between devices, body(): lax.psum((weight_terms[0], weight_terms[1]), 'rows')  105 us
    psum x1, waiting for transfers between devices, body(): lax.psum(lax.psum((weight_terms[0], weight_terms[1]), 'rows'), 'cols')  60.4 us
    all_gather x1, waiting for transfers between devices, body(): rows_in = lax.all_gather(grad_pre, 'cols', axis=0, tiled=True)  46.1 us
    dot_general x1, matrix products, body(): jnp.dot(pick_table, per_ref.reshape(blocks * per_block, tile_rows * feat_...  42.4 us
    dot_general x1, local copies, waits for them, and re-layouts, body(): jnp.einsum('bkij,bif->bkjf', adj_vals, grad_blocks, preferred_element_typ...  33.4 us
    all_to_all x1, waiting for transfers between devices, body(): lax.all_to_all(outgoing, 'rows', split_axis=0, concat_axis=0, tiled=True)  29.7 us
    all_to_all x1, waiting for transfers between devices, body(): lax.all_to_all(remote_shares, 'rows', split_axis=0, concat_axis=0, tiled=...  25.6 us
    dot_general x1, matrix products, body(): jnp.einsum('bkij,bif->bkjf', adj_vals, grad_blocks, preferred_element_typ...  21.4 us
  transfers between devices with their start and end apart: 8, of which 7 were waited for; matrix products, arithmetic and copies ran while one was open for 9% of the time, Pallas kernels for 0%

profile of v1, /device:TPU:0, one launch (start us, length us, event | category | flops | bytes accessed | tf_op | source)
XLA Modules:
  0.0 505.0 jit_solution(9500874507125019641)
XLA Ops:
  8.6 7.4 %all-to-all-start.1 = ((s32[1,32,2]{2,0,1:T(1,128)}), s32[1,32,2]{2,0,1:T(1,128)S(1)}, u32[]{:S(2)}, u32[]{:S(2)}) async-start(s32[1,32,2]{2,0,1:T(1,128)} %copy.40), calls=%async_computation.1 | async-start | bytes 32768 | tf_op jit(solution)/shard_map/all_to_all | solution.py:17
  17.5 5.7 %all-to-all-done.1 = s32[1,32,2]{2,0,1:T(1,128)S(1)} async-done(((s32[1,32,2]{2,0,1:T(1,128)}), s32[1,32,2]{2,0,1:T(1,128)S(1)}, u32[]{:S(2)}, u32[]{:S(2)}) %all-to-all-start.1) | async-done | bytes 288 | tf_op jit(solution)/shard_map/all_to_all | solution.py:17
  25.4 1.9 copy.54
  27.3 4.1 all-to-all-start.2
  31.7 29.7 %all-to-all-done.2 = bf16[32,2,128,128]{3,2,1,0:T(8,128)(2,1)S(1)} async-done(((bf16[32,2,128,128]{3,2,1,0:T(8,128)(2,1)}), bf16[32,2,128,128]{3,2,1,0:T(8,128)(2,1)S(1)}, u32[]{:S(2)}, u32[]{:S(2)}) %all-to-all-start.2) | async-done | bytes 2097184 | tf_op jit(solution)/shard_map/all_to_all | solution.py:23
  61.4 5.3 %all-to-all-start = ((bf16[4,1024,128]{2,1,0:T(8,128)(2,1)}), bf16[4,1024,128]{2,1,0:T(8,128)(2,1)}, u32[]{:S(2)}, u32[]{:S(2)}) async-start(bf16[4,1024,128]{2,1,0:T(8,128)(2,1)} %bitcast), calls=%async_computation | async-start | bytes 2097152 | tf_op jit(solution)/shard_map/all_to_all | solution.py:35
  66.7 3.2 pad_maximum_fusion
  69.9 15.8 %gather_fusion = bf16[512,128,128]{2,1,0:T(8,128)(2,1)} fusion(bf16[96,128,128]{2,1,0:T(8,128)(2,1)} %pad_maximum_fusion, s32[1024]{0:T(1024)S(1)} %pad_clamp_fusion), kind=kCustom, calls=%fused_computation | custom fusion | bytes 33556480 | tf_op jit(solution)/shard_map/jit(_take)/gather | solution.py:31
  85.7 13.0 %bitcast_convert_fusion = bf16[32,128,128]{1,2,0:T(8,128)(2,1)S(1)} fusion(bf16[32,16,128,128]{3,2,1,0:T(8,128)(2,1)} %param.8, bf16[32,16,128,128]{3,2,1,0:T(8,128)(2,1)} %bitcast.60, pred[32,16]{1,0:T(8,128)(4,1)S(1)} %copy.39), kind=kOutput, calls=%fused_computation.35 | convolution fusion | flops 2156396544 | bytes 34603520 | tf_op jit(solution)/shard_map/bkij,bkjf->bif/dot_general | solution.py:32
  100.0 4.9 all-to-all-start.3
  106.4 2.1 fusion.37
  108.5 9.3 %all-to-all-done.3 = bf16[4,1024,128]{1,2,0:T(8,128)(2,1)S(1)} async-done(((bf16[4,1024,128]{1,2,0:T(8,128)(2,1)}), bf16[4,1024,128]{1,2,0:T(8,128)(2,1)S(1)}, u32[]{:S(2)}, u32[]{:S(2)}) %all-to-all-start.3) | async-done | bytes 1048608 | tf_op jit(solution)/shard_map/all_to_all | solution.py:36
  118.8 5.4 %fusion.15 = (bf16[1024,512]{1,0:T(8,128)(2,1)S(1)}, bf16[1024,512]{1,0:T(8,128)(2,1)}) fusion(bf16[1024,512]{1,0:T(8,128)(2,1)} %param.13, f32[1024,512]{1,0:T(8,128)} %fusion.37, bf16[1024,512]{0,1:T(8,128)(2,1)} %bitcast.66, bf16[512,512]{1,0:T(8,128)(2,1)S(1)} %copy-done), kind=kOutput, calls=%fused_computation.23 | convolution fusion | flops 549453824 | bytes 6815744 | tf_op jit(solution)/shard_map/dot_general | solution.py:38
  124.2 1.7 convolution_bitcast_fusion.1
  125.9 1.7 fusion.38
  127.7 104.8 %all-reduce.5.cloned.1.call-done = (f32[512,512]{0,1:T(8,128)}, f32[512,512]{0,1:T(8,128)}) async-done(((f32[512,512]{0,1:T(8,128)}, f32[512,512]{0,1:T(8,128)}), (f32[512,512]{0,1:T(8,128)}, f32[512,512]{0,1:T(8,128)})) %all-reduce.5.cloned.1.call-update) | async-done | bytes 2097168 | tf_op jit(solution)/shard_map/psum | solution.py:48
  233.4 60.4 %all-reduce.7.cloned.1.call-done = (f32[512,512]{0,1:T(8,128)}, f32[512,512]{0,1:T(8,128)}) async-done(((f32[512,512]{0,1:T(8,128)}, f32[512,512]{0,1:T(8,128)}), (f32[512,512]{0,1:T(8,128)}, f32[512,512]{0,1:T(8,128)})) %all-reduce.7.cloned.1.call-update) | async-done | bytes 2097168 | tf_op jit(solution)/shard_map/psum | solution.py:48
  293.8 1.8 broadcast_multiply_fusion
  298.2 46.1 %all-gather.2.cloned.1.call-done = bf16[4096,512]{1,0:T(8,128)(2,1)} async-done(((bf16[1024,512]{1,0:T(8,128)(2,1)}), bf16[4096,512]{1,0:T(8,128)(2,1)}) %all-gather.2.cloned.1.call-update) | async-done | bytes 4194320 | tf_op jit(solution)/shard_map/all_gather | solution.py:56
  344.3 3.4 convolution_convert_fusion.1
  347.8 21.4 %convolution_bitcast_fusion = f32[32,16,128,128]{2,3,1,0:T(8,128)} fusion(bf16[32,128,128,1]{2,1,3,0:T(8,128)(2,1)S(1)} %bitcast.63, bf16[32,16,128,128]{3,2,1,0:T(8,128)(2,1)} %param.8), kind=kOutput, calls=%fused_computation.9 | convolution fusion | flops 2147483648 | bytes 51380224 | tf_op jit(solution)/shard_map/bkij,bif->bkjf/dot_general | solution.py:65
  369.1 33.4 %copy.46 = f32[32,16,128,128]{3,2,1,0:T(8,128)} copy(f32[32,16,128,128]{2,3,1,0:T(8,128)} %convolution_bitcast_fusion) | data formatting | bytes 67108864 | tf_op jit(solution)/shard_map/bkij,bif->bkjf/dot_general | solution.py:65
  402.6 42.4 %fusion.3 = bf16[96,16384]{1,0:T(8,128)(2,1)} fusion(f32[64,8,128,128]{3,2,1,0:T(8,128)} %bitcast.59, s32[512]{0:T(512)S(1)} %eq.35), kind=kOutput, calls=%fused_computation.4 | convolution fusion | flops 9665298432 | bytes 36702208 | tf_op jit(solution)/shard_map/dot_general | solution.py:72
  445.0 1.7 slice_bitcast_fusion
  446.8 1.9 copy.56
  448.7 7.2 %all-to-all-start.4 = ((bf16[32,2,128,128]{3,2,1,0:T(8,128)(2,1)}), bf16[32,2,128,128]{3,2,1,0:T(8,128)(2,1)}, u32[]{:S(2)}, u32[]{:S(2)}) async-start(bf16[32,2,128,128]{3,2,1,0:T(8,128)(2,1)} %bitcast.29), calls=%async_computation.4 | async-start | bytes 4194304 | tf_op jit(solution)/shard_map/all_to_all | solution.py:80
  455.9 2.7 slice_convert_fusion
  458.6 1.7 reshape.72
  460.3 25.6 %all-to-all-done.4 = bf16[32,2,128,128]{3,2,1,0:T(8,128)(2,1)} async-done(((bf16[32,2,128,128]{3,2,1,0:T(8,128)(2,1)}), bf16[32,2,128,128]{3,2,1,0:T(8,128)(2,1)}, u32[]{:S(2)}, u32[]{:S(2)}) %all-to-all-start.4) | async-done | bytes 2097184 | tf_op jit(solution)/shard_map/all_to_all | solution.py:80
  485.9 4.4 fusion.23
  490.3 2.7 reshape.71
  493.0 5.5 %fusion.12 = f32[4096,128]{1,0:T(8,128)} fusion(f32[4096,128]{1,0:T(8,128)} %reshape.71, f32[4096,128]{1,0:T(8,128)S(1)} %reshape.72, bf16[4096,512]{1,0:T(8,128)(2,1)} %all-gather.2.cloned.1.call-done, bf16[512,512]{1,0:T(8,128)(2,1)S(1)} %copy-done.5, s32[]{:T(128)S(6)} %select_n.15), kind=kOutput, calls=%fused_computation.15 | convolution fusion | flops 538968064 | bytes 10616836 | tf_op jit(solution)/shard_map/dot_general | solution.py:57
  (39 shorter events, 12.6 us)
Async XLA Ops:
  7.2 111.6 %copy-start = (bf16[512,512]{1,0:T(8,128)(2,1)S(1)}, bf16[512,512]{1,0:T(8,128)(2,1)}, u32[]{:S(2)}) copy-start(bf16[512,512]{1,0:T(8,128)(2,1)} %param.12) | copy-start | bytes 1572868
  8.6 14.7 %all-to-all-start.1 = ((s32[1,32,2]{2,0,1:T(1,128)}), s32[1,32,2]{2,0,1:T(1,128)S(1)}, u32[]{:S(2)}, u32[]{:S(2)}) async-start(s32[1,32,2]{2,0,1:T(1,128)} %copy.40), calls=%async_computation.1 | async-start | bytes 32768 | tf_op jit(solution)/shard_map/all_to_all | solution.py:17
  27.3 4.2 copy-start.6
  27.3 34.1 %all-to-all-start.2 = ((bf16[32,2,128,128]{3,2,1,0:T(8,128)(2,1)}), bf16[32,2,128,128]{3,2,1,0:T(8,128)(2,1)S(1)}, u32[]{:S(2)}, u32[]{:S(2)}) async-start(bf16[32,2,128,128]{3,2,1,0:T(8,128)(2,1)} %bitcast.62), calls=%async_computation.2 | async-start | bytes 4194304 | tf_op jit(solution)/shard_map/all_to_all | solution.py:23
  61.4 38.6 %all-to-all-start = ((bf16[4,1024,128]{2,1,0:T(8,128)(2,1)}), bf16[4,1024,128]{2,1,0:T(8,128)(2,1)}, u32[]{:S(2)}, u32[]{:S(2)}) async-start(bf16[4,1024,128]{2,1,0:T(8,128)(2,1)} %bitcast), calls=%async_computation | async-start | bytes 2097152 | tf_op jit(solution)/shard_map/all_to_all | solution.py:35
  100.0 6.4 %copy-start.5 = (bf16[512,512]{1,0:T(8,128)(2,1)S(1)}, bf16[512,512]{1,0:T(8,128)(2,1)}, u32[]{:S(2)}) copy-start(bf16[512,512]{1,0:T(8,128)(2,1)} %param.11) | copy-start | bytes 1572868
  100.0 17.8 %all-to-all-start.3 = ((bf16[4,1024,128]{1,2,0:T(8,128)(2,1)}), bf16[4,1024,128]{1,2,0:T(8,128)(2,1)S(1)}, u32[]{:S(2)}, u32[]{:S(2)}) async-start(bf16[4,1024,128]{1,2,0:T(8,128)(2,1)} %copy.42), calls=%async_computation.3 | async-start | bytes 2097152 | tf_op jit(solution)/shard_map/all_to_all | solution.py:36
  104.9 127.6 %all-reduce.5.cloned.1.call-start = ((), (), s32[]{:S(2)}) async-start(), calls=%async_computation.6 | async-start | bytes 4194304 | tf_op jit(solution)/shard_map/psum | solution.py:48
  117.8 1.0 copy-start.3
  124.1 3.5 copy-start.2
  124.2 1.7 copy-start.4
  127.6 166.2 %all-reduce.7.cloned.1.call-start = ((), (), s32[]{:S(2)}) async-start(), calls=%async_computation.7 | async-start | bytes 4194304 | tf_op jit(solution)/shard_map/psum | solution.py:48
  232.5 111.8 %all-gather.2.cloned.1.call-start = ((), (), s32[]{:S(2)}) async-start(), calls=%async_computation.5 | async-start | bytes 5242880 | tf_op jit(solution)/shard_map/all_gather | solution.py:56
  448.7 37.2 %all-to-all-start.4 = ((bf16[32,2,128,128]{3,2,1,0:T(8,128)(2,1)}), bf16[32,2,128,128]{3,2,1,0:T(8,128)(2,1)}, u32[]{:S(2)}, u32[]{:S(2)}) async-start(bf16[32,2,128,128]{3,2,1,0:T(8,128)(2,1)} %bitcast.29), calls=%async_computation.4 | async-start | bytes 4194304 | tf_op jit(solution)/shard_map/all_to_all | solution.py:80
  493.0 5.5 %copy-start.1 = (bf16[512,512]{1,0:T(8,128)(2,1)S(1)}, bf16[512,512]{1,0:T(8,128)(2,1)}, u32[]{:S(2)}) copy-start(bf16[512,512]{1,0:T(8,128)(2,1)} %param.12) | copy-start | bytes 1572868
Sparse Core Ops, SparseCore 0:
  127.8 104.6 all-reduce.4
  234.9 58.8 all-reduce.6
  296.2 48.1 all-gather.1
